TPU v7x, 512 devices: a whole 4x4x16 slice. The times are simulated.
512 devices in a mesh: subj: 16 (over y, z_hi), vox: 32 (over z_lo, x, core).
Axes of the slice: x: 4, y: 4, z: 16 (z_hi: 4, z_lo: 4; z = z_hi * 4 + z_lo), core: 2. Of those that a mesh axis runs over, the one named last changes fastest.
Arguments:
- contrasts: bfloat16 [1792, 64, 9919], P('subj', 'vox'), may hold values from -60 to 60
- flips: int32 [48, 1792], P(None, 'subj'), may hold values from -1 to 1, as said below
- mask: int32 [64, 9919], P('vox'), may hold values 0 or 1
Outputs:
- highest: float32 [64, 9919], P('vox')
- exceed: float32 [64, 9919], P('vox')
Inputs may be any that keep to these rules, and one draw needn't show every extreme that they name: `flips`: every entry is -1 or +1.
All inputs are finite; a program needn't handle non-finite values. No bound on the sum of `mask` on one device may be relied on, other than what follows from the above.
Results may differ from a plain program's by a relative error of at most 0.0003.
Values sent between devices are 32-bit elements; how exact they have to be, the bound alone decides.
A program may use at most 64 MiB of HBM per device.

v0:
```python
import math

import jax
import jax.numpy as jnp
from jax import lax
from jax.sharding import PartitionSpec as P

PY = 109
RADIUS = 2
FB = 16
NB = 3
NF = 48


epsilon = 1e-06


def padded_2(shard, sides, width):
    for axis, dim in sides:
        size, length = (lax.axis_size(axis), shard.shape[dim])
        up = [(i, (i + 1) % size) for i in range(size - 1)]
        down = [(j, i) for i, j in up]
        last = lax.slice_in_dim(shard, length - width, length, axis=dim)
        leading = lax.slice_in_dim(shard, 0, width, axis=dim)
        before = lax.ppermute(last, axis, up)
        after = lax.ppermute(leading, axis, down)
        shard = jnp.concatenate([before, shard, after], axis=dim)
    return shard


def along_plane(volume, stride):
    margin = RADIUS * stride
    widths = [(0, 0)] * (volume.ndim - 1) + [(margin, margin)]
    padded = jnp.pad(volume, widths)
    length = volume.shape[-1]
    column = jnp.arange(length) % PY
    result = jnp.zeros(volume.shape, jnp.float32)
    for offset in range(-RADIUS, RADIUS + 1):
        begin = margin + offset * stride
        shifted = padded[..., begin : begin + length]
        if stride == 1:
            inside = (column + offset >= 0) & (column + offset < PY)
            shifted = jnp.where(inside, shifted, jnp.zeros_like(shifted))
        result = result + math.exp(-0.5 * offset * offset) * shifted
    return result


def depth_weights(positions, total):
    result = jnp.zeros(positions.shape, jnp.float32)
    for offset in range(-RADIUS, RADIUS + 1):
        inside = ((positions + offset >= 0) & (positions + offset < total)).astype(jnp.float32)
        result = result + math.exp(-0.5 * offset * offset) * inside
    return result


def smooth(volume, norm_all):
    flat = along_plane(along_plane(volume, 1), PY)
    padded = padded_2(flat, (("vox", 1),), RADIUS)
    depth = volume.shape[1]
    summed = jnp.zeros(volume.shape, jnp.float32)
    for offset in range(-RADIUS, RADIUS + 1):
        summed = (
            summed
            + math.exp(-0.5 * offset * offset)
            * padded[:, RADIUS + offset : RADIUS + offset + depth]
        )
    return summed / norm_all


def per_device(contrasts, flips, mask):
    local_subjects, depth, plane_cells = contrasts.shape
    groups = lax.axis_size("subj")
    number = jnp.float32(local_subjects * groups)
    values = contrasts.reshape(local_subjects, depth * plane_cells)
    unity = jnp.ones((1, local_subjects), jnp.bfloat16)
    linear = jnp.dot(unity, values, preferred_element_type=jnp.float32)[0]
    squared = jnp.sum(jnp.square(values.astype(jnp.float32)), axis=0)
    linear, second = lax.psum((linear, squared), "subj")
    positions = lax.axis_index("vox") * depth + jnp.arange(depth, dtype=jnp.int32)
    depth_norm = depth_weights(positions, depth * lax.axis_size("vox"))
    plane_norm = along_plane(along_plane(jnp.ones((plane_cells,), jnp.float32), 1), PY)
    norm_all = plane_norm[None, None, :] * depth_norm[None, :, None]
    second = second.reshape(1, depth, plane_cells)
    sigma = jnp.sqrt(smooth(second / number, norm_all) + epsilon)[0]
    denominator = jnp.sqrt(number) * sigma
    observed = linear.reshape(depth, plane_cells) / denominator
    highest = jnp.full((depth, plane_cells), -1e30, jnp.float32)
    exceed = jnp.zeros((depth, plane_cells), jnp.float32)
    for batch_index in range(NB):
        sign_rows = flips[batch_index * FB : (batch_index + 1) * FB].astype(jnp.bfloat16)
        partial_value = jnp.dot(sign_rows, values, preferred_element_type=jnp.float32)
        block_sums = lax.psum(partial_value, "subj")
        tflip = block_sums.reshape(-1, depth, plane_cells) / denominator[None]
        highest = jnp.maximum(highest, jnp.max(tflip, axis=0))
        exceed = exceed + jnp.sum(jax.nn.sigmoid(2.0 * (tflip - observed[None])), axis=0)
    inside = mask.astype(jnp.float32)
    return (highest * inside, exceed / NF * inside)


def solution(mesh):
    in_specs = (P("subj", "vox", None), P(None, "subj"), P("vox", None))
    out_specs = (P("vox", None), P("vox", None))
    return jax.shard_map(
        per_device, mesh=mesh, in_specs=in_specs, out_specs=out_specs, check_vma=False
    )
```

profile of v0, /device:TPU:6, one launch (start us, length us, event | category | flops | bytes accessed | tf_op | source)
XLA Modules:
  0.0 453.9 jit_solution(17871860759071966162)
XLA Ops:
  7.2 0.0 copy-start.3
  7.2 0.0 all-reduce.7.cloned.1.call-start
  7.2 8.1 %reshape.174 = bf16[112,19838]{1,0:T(8,128)(2,1)} reshape(bf16[112,2,9919]{2,1,0:T(2,128)(2,1)} %param.3) | data formatting | bytes 8887424 | tf_op jit(solution)/shard_map/reshape | solution.py:74
  15.3 0.0 copy-done.3
  15.3 0.0 copy-start
  15.3 4.2 fusion.58
  19.4 0.0 copy-done
  19.4 0.0 slice-start
  19.5 1.8 fusion.60
  21.2 0.0 slice-start.1
  21.2 1.8 fusion.62
  23.0 0.7 convolution_reduce_fusion
  23.7 0.0 slice-done
  23.7 0.0 slice-done.1
  23.7 4.7 %multiply_reduce_fusion = f32[2,9919]{1,0:T(2,128)S(1)} fusion(bf16[112,2,9919]{2,1,0:T(2,128)(2,1)S(1)} %bitcast.5), kind=kLoop, calls=%fused_computation | loop fusion | flops 6645730 | bytes 4523064 | tf_op jit(solution)/shard_map/reduce_sum | solution.py:77
  28.4 0.7 reshape.175
  29.1 0.7 reduce_sum.39
  29.9 0.0 all-reduce.7.cloned.1.call-update
  30.1 0.1 fusion.29
  30.2 0.1 fusion.20
  30.3 400.5 %all-reduce.7.cloned.1.call-done = (f32[1,2,9919]{2,1,0:T(2,128)}, f32[19838]{0:T(1024)}, f32[16,19838]{1,0:T(8,128)}, f32[16,19838]{1,0:T(8,128)}, f32[16,19838]{1,0:T(8,128)}) async-done(((f32[1,2,9919]{2,1,0:T(2,128)}, f32[19838]{0:T(1024)}, f32[16,19838]{1,0:T(8,128)}, f32[16,19838]{1,0:T(8,128)}, f32[16,19838]{1,0:T(8,128)}), (f32[1,2,9919]{2,1,0:T(2,128)}, f32[19838]{0:T(1024)}, ...) | async-done | bytes 3967616 | tf_op jit(solution)/shard_map/psum | solution.py:78
  430.8 0.0 copy-start.1
  430.8 1.0 broadcast_multiply_fusion
  431.8 0.1 div.65
  432.0 0.4 multiply_add_fusion.1
  432.4 0.4 multiply_add_fusion
  432.8 1.9 collective-permute-start
  434.7 3.8 collective-permute-start.1
  438.6 0.0 collective-permute-done
  438.6 1.8 collective-permute-done.1
  440.4 1.3 fusion.70
  441.6 0.1 div.67
  441.8 0.1 sub.25
  441.9 0.0 copy-done.1
  441.9 0.0 copy-start.2
  441.9 4.1 fusion.1
  446.0 0.1 max.12
  446.2 0.1 div.78
  446.3 0.0 copy-done.2
  446.3 0.7 convert_multiply_fusion
  (9 shorter events, 0.2 us)
Async XLA Ops:
  7.2 8.1 %copy-start.3 = (s32[48,112]{1,0:T(8,128)S(1)}, s32[48,112]{1,0:T(8,128)}, u32[]{:S(2)}) copy-start(s32[48,112]{1,0:T(8,128)} %param.4) | copy-start | bytes 64516
  7.2 423.7 %all-reduce.7.cloned.1.call-start = ((), (), s32[]{:S(2)}) async-start(), calls=%async_computation | async-start | bytes 7942144 | tf_op jit(solution)/shard_map/psum | solution.py:78
  15.3 4.2 copy-start
  19.4 4.2 slice-start
  21.2 2.5 slice-start.1
  430.8 11.1 %copy-start.1 = (f32[16,19838]{1,0:T(8,128)S(1)}, f32[16,19838]{1,0:T(8,128)}, u32[]{:S(2)}) copy-start(f32[16,19838]{1,0:T(8,128)} %get-tuple-element.14) | copy-start | bytes 3808900
  432.8 5.8 %collective-permute-start = (f32[1,2,9919]{2,1,0:T(2,128)S(1)}, f32[1,2,9919]{2,1,0:T(2,128)S(1)}, u32[]{:S(2)}, u32[]{:S(2)}) collective-permute-start(f32[1,2,9919]{2,1,0:T(2,128)S(1)} %multiply_add_fusion), channel_id=1, source_target_pairs={{0,1},{1,2},{2,3},{3,4},{4,5},{5,6},{6,7},{7,8},{8,9},{9,10},{10,1... | collective-permute-start | bytes 238064 | tf_op jit(solution)/shard_map/ppermute | solution.py:25
  434.7 5.7 %collective-permute-start.1 = (f32[1,2,9919]{2,1,0:T(2,128)S(1)}, f32[1,2,9919]{2,1,0:T(2,128)S(1)}, u32[]{:S(2)}, u32[]{:S(2)}) collective-permute-start(f32[1,2,9919]{2,1,0:T(2,128)S(1)} %multiply_add_fusion), channel_id=1, source_target_pairs={{1,0},{2,1},{3,2},{4,3},{5,4},{6,5},{7,6},{8,7},{9,8},{10,9},{11,1... | collective-permute-start | bytes 238064 | tf_op jit(solution)/shard_map/ppermute | solution.py:26
  441.9 4.4 copy-start.2
Sparse Core Ops, SparseCore 0:
  30.0 400.7 all-reduce.6
where the time goes:
time: 460 us; the launch traced here: 454 us
  waiting for transfers between devices  402 us (87%)
  between operations  14.2 us (3%)
  other arithmetic  12.9 us (3%)
  local copies, waits for them, and re-layouts  10.2 us (2%)
  matrix products  8.38 us (2%)
  starting transfers between devices  5.78 us (1%)
    psum x1, waiting for transfers between devices, per_device(): linear, second = lax.psum((linear, squared), 'subj')  401 us
  transfers between devices with their start and end apart: 3, of which 2 were waited for; matrix products, arithmetic and copies ran while one was open for 0% of the time, Pallas kernels for 0%

commit v1 on v0

v1 whole, which is shorter than its diff:
```python
import functools
import math

import jax
import jax.numpy as jnp
from jax import lax
from jax.experimental import pallas as pl
from jax.experimental.pallas import tpu as pltpu
from jax.sharding import PartitionSpec as P

NX = 91
PY = 109
PLANE = NX * PY
NZ = 64
NF = 48
SUBJ = 1792
RADIUS = 2
EPSILON = 1e-06

LANES = 640
PIECES = 16
WIDE = LANES * PIECES
PAIR = 2 * LANES
BLOCK = 256
GROUP = 8
CHUNKS = NF // GROUP
EXTRA = CHUNKS
MARGIN = 256
ORDER = (0, 1, 2, EXTRA, 3, 4, 5)

WEIGHT = {k: math.exp(-0.5 * k * k) for k in range(-RADIUS, RADIUS + 1)}
MESH = pl.DeviceIdType.MESH


def row_of(position):
    return (position * 38480) >> 22


def first_bit(i):
    return ((i + 1) // 2) % 2


def second_bit(i):
    return i // 2


def partner(i, kind):
    odd = i % 2
    return (i + 1 - 2 * odd) if kind == 0 else (i + 3 + 2 * odd) % 4


def kernel(
    x_hbm, flips_ref, high_ref, exceed_ref,
    x, w, full, extra, r1, r2, r3, r4, e1, e2, e3, e4, s2, s3, s4, t2, t3, t4,
    square, swept, smooth, before, after, gathered,
    in_sem, send_sem, recv_sem, halo_send, halo_recv, gather_send, gather_recv,
):
    subj = lax.axis_index("subj")
    vox = lax.axis_index("vox")
    n_vox = lax.axis_size("vox")
    y, z = subj // 4, subj % 4
    up = (vox + 1) % n_vox
    down = (vox + n_vox - 1) % n_vox

    def y_peer(kind):
        return {"subj": partner(y, kind) * 4 + z}

    def z_peer(kind):
        return {"subj": y * 4 + partner(z, kind)}

    loads = []
    for j in range(8):
        stop = min(PAIR * (j + 1), PLANE)
        view = (slice(None), slice(None), pl.ds(PAIR * j, stop - PAIR * j))
        load = pltpu.make_async_copy(x_hbm.at[view], x.at[view], in_sem.at[j])
        load.start()
        loads.append(load)

    barrier = pltpu.get_barrier_semaphore()
    for kind in range(2):
        pl.semaphore_signal(barrier, 1, device_id=y_peer(kind), device_id_type=MESH)
        pl.semaphore_signal(barrier, 1, device_id=z_peer(kind), device_id_type=MESH)
    for other in (up, down):
        pl.semaphore_signal(barrier, 1, device_id={"vox": other}, device_id_type=MESH)

    signs = flips_ref[...].astype(jnp.float32).astype(jnp.bfloat16)
    n_local = signs.shape[1]
    column = lax.broadcasted_iota(jnp.int32, (n_local, 2 * n_local), 1)
    subject = lax.broadcasted_iota(jnp.int32, (n_local, 2 * n_local), 0)
    for p in range(2):
        spread = (column == 2 * subject + p).astype(jnp.float32).astype(jnp.bfloat16)
        w[pl.ds(NF * p, NF), :] = jnp.dot(
            signs, spread, preferred_element_type=jnp.float32
        ).astype(jnp.bfloat16)
    lane = lax.broadcasted_iota(jnp.int32, (16, 2 * n_local), 1)
    line = lax.broadcasted_iota(jnp.int32, (16, 2 * n_local), 0)
    w[pl.ds(2 * NF, 16), :] = (lane % 2 == line).astype(jnp.float32).astype(jnp.bfloat16)

    square[:, pl.ds(0, MARGIN)] = jnp.zeros((2, MARGIN), jnp.float32)
    square[:, pl.ds(MARGIN + WIDE - LANES, LANES + MARGIN)] = jnp.zeros((2, LANES + MARGIN), jnp.float32)
    swept[:, pl.ds(0, MARGIN)] = jnp.zeros((2, MARGIN), jnp.float32)
    swept[:, pl.ds(MARGIN + WIDE, MARGIN)] = jnp.zeros((2, MARGIN), jnp.float32)
    for p in range(2):
        for g in range(CHUNKS):
            full[p, g, PIECES - 1] = jnp.zeros((GROUP, LANES), jnp.float32)
        extra[p, PIECES - 1] = jnp.zeros((2, LANES), jnp.float32)

    def block(start, width, piece_of):
        values = x[:, :, pl.ds(start, width)].reshape(2 * n_local, width)
        sums = jnp.dot(w[...], values, preferred_element_type=jnp.float32)
        wide = values.astype(jnp.float32)
        squared = jnp.sum((wide * wide).reshape(n_local // 4, 8, width), axis=0)
        second = squared[0:2] + squared[2:4] + squared[4:6] + squared[6:8]
        square[:, pl.ds(MARGIN + start, width)] = second
        for part in range(2):
            low = 128 * part
            size = min(128, width - low)
            piece, offset = piece_of(part)
            place = pl.ds(offset, size)
            for p in range(2):
                for g in range(CHUNKS):
                    row = NF * p + GROUP * g
                    full[p, g, piece, :, place] = sums[row:row + GROUP, low:low + size]
                row = 2 * NF + p
                extra[p, piece, pl.ds(0, 1), place] = sums[row:row + 1, low:low + size]

    def pair(j, count, last_width):
        base = pl.multiple_of(j * PAIR, 128) if not isinstance(j, int) else j * PAIR
        for i in range(count):
            def piece_of(part, i=i):
                tile = 2 * i + part
                return 2 * j + tile // 5, 128 * (tile % 5)
            block(base + BLOCK * i, last_width if i == count - 1 else BLOCK, piece_of)

    for j in range(7):
        loads[j].wait()

    @pl.loop(0, 7)
    def _(j):
        pair(j, 5, BLOCK)

    loads[7].wait()
    rest = PLANE - 7 * PAIR
    pair(7, pl.cdiv(rest, BLOCK), rest - BLOCK * (pl.cdiv(rest, BLOCK) - 1))

    pl.semaphore_wait(barrier, 6)

    keep = []
    for p in range(2):
        bits = (first_bit, second_bit) if p == 0 else (second_bit, first_bit)
        keep.append([bits[0](y), bits[1](y), bits[0](z), bits[1](z)])

    def send_of(step, p, c):
        k1 = keep[p][0]
        if c == EXTRA:
            source = [extra.at[p, pl.ds(8 * (1 - k1), 8)], t2.at[p], t3.at[p], t4.at[p]][step]
            target = [e1, e2, e3, e4][step].at[p]
        else:
            source = [full.at[p, c, pl.ds(8 * (1 - k1), 8)], s2.at[p, c], s3.at[p, c], s4.at[p, c]][step]
            target = [r1, r2, r3, r4][step].at[p, c]
        peer = [y_peer(p), y_peer(1 - p), z_peer(p), z_peer(1 - p)][step]
        return pltpu.make_async_remote_copy(
            src_ref=source, dst_ref=target,
            send_sem=send_sem.at[step, p, c], recv_sem=recv_sem.at[step, p, c],
            device_id=peer, device_id_type=MESH,
        )

    def views(p, c):
        if c == EXTRA:
            return extra.at[p], e1.at[p], e2.at[p], e3.at[p], e4.at[p]
        return full.at[p, c], r1.at[p, c], r2.at[p, c], r3.at[p, c], r4.at[p, c]

    started = []

    def start(step, c):
        for p in range(2):
            copy = send_of(step, p, c)
            copy.start()
            started.append(copy)

    def advance(step, c):
        for p in range(2):
            k1, k2, k3, k4 = keep[p]
            send_of(step, p, c).wait_recv()
            a, b1, b2, b3, _ = views(p, c)
            if step == 0:
                out = t2.at[p] if c == EXTRA else s2.at[p, c]
                for i in range(4):
                    at = 4 * (1 - k2) + i
                    out[i] = a[8 * k1 + at] + b1[at]
            elif step == 1:
                out = t3.at[p] if c == EXTRA else s3.at[p, c]
                for i in range(2):
                    at = 2 * (1 - k3) + i
                    out[i] = a[8 * k1 + 4 * k2 + at] + b1[4 * k2 + at] + b2[at]
            elif step == 2:
                out = t4.at[p] if c == EXTRA else s4.at[p, c]
                at = 1 - k4
                out[0] = a[8 * k1 + 4 * k2 + 2 * k3 + at] + b1[4 * k2 + 2 * k3 + at] + b2[2 * k3 + at] + b3[at]
            copy = send_of(step + 1, p, c)
            copy.start()
            started.append(copy)

    def total(p, c):
        k1, k2, k3, k4 = keep[p]
        a, b1, b2, b3, b4 = views(p, c)
        return a[8 * k1 + 4 * k2 + 2 * k3 + k4] + b1[4 * k2 + 2 * k3 + k4] + b2[2 * k3 + k4] + b3[k4] + b4[0]

    start(0, ORDER[0])
    start(0, ORDER[1])

    SEG = 1280

    def shifted(ref, base, offset):
        padded = ref[:, pl.ds(base, SEG + 2 * MARGIN)]
        return pltpu.roll(padded, (-offset) % (SEG + 2 * MARGIN), 1)[:, MARGIN:MARGIN + SEG]

    @pl.loop(0, WIDE // SEG)
    def _(i):
        base = pl.multiple_of(i * SEG, 128)
        position = base + lax.broadcasted_iota(jnp.int32, (2, SEG), 1)
        at = position - PY * row_of(position)
        result = jnp.zeros((2, SEG), jnp.float32)
        for k in range(-RADIUS, RADIUS + 1):
            moved = shifted(square, base, k)
            inside = (at + k >= 0) & (at + k < PY)
            result = result + WEIGHT[k] * jnp.where(inside, moved, 0.0)
        swept[:, pl.ds(pl.multiple_of(base + MARGIN, 128), SEG)] = result

    @pl.loop(0, WIDE // SEG)
    def _(i):
        base = pl.multiple_of(i * SEG, 128)
        result = jnp.zeros((2, SEG), jnp.float32)
        for k in range(-RADIUS, RADIUS + 1):
            result = result + WEIGHT[k] * shifted(swept, base, k * PY)
        smooth[:, pl.ds(base, SEG)] = result

    halo = [
        pltpu.make_async_remote_copy(
            src_ref=smooth, dst_ref=target, send_sem=halo_send.at[i], recv_sem=halo_recv.at[i],
            device_id={"vox": other}, device_id_type=MESH,
        )
        for i, (target, other) in enumerate(((before, up), (after, down)))
    ]
    for copy in halo:
        copy.start()

    def depth():
        for copy in halo:
            copy.wait_recv()
        first = vox > 0
        last = vox < n_vox - 1
        for i in range(PIECES):
            place = pl.ds(LANES * i, LANES)
            lower = jnp.where(first, before[:, place], 0.0)
            upper = jnp.where(last, after[:, place], 0.0)
            own = smooth[:, place]
            extra[0, i, pl.ds(1, 1), :] = (
                WEIGHT[2] * lower[0:1] + WEIGHT[1] * lower[1:2] + own[0:1] + WEIGHT[1] * own[1:2] + WEIGHT[2] * upper[0:1]
            )
            extra[1, i, pl.ds(1, 1), :] = (
                WEIGHT[2] * lower[1:2] + WEIGHT[1] * own[0:1] + own[1:2] + WEIGHT[1] * upper[0:1] + WEIGHT[2] * upper[1:2]
            )

    n = len(ORDER)
    for t in range(n + 4):
        if t < n:
            advance(0, ORDER[t])
            if t + 2 < n:
                if ORDER[t + 2] == EXTRA:
                    depth()
                start(0, ORDER[t + 2])
        if 0 <= t - 1 < n:
            advance(1, ORDER[t - 1])
        if 0 <= t - 3 < n:
            advance(2, ORDER[t - 3])

    number = jnp.float32(SUBJ)

    def wait_last(c):
        for p in range(2):
            send_of(3, p, c).wait_recv()

    for c in ORDER:
        wait_last(c)

    owned = []
    for p in range(2):
        k1, k2, k3, k4 = keep[p]
        piece = 8 * k1 + 4 * k2 + 2 * k3 + k4
        owned.append(piece)
        position = piece * LANES + lax.broadcasted_iota(jnp.int32, (1, LANES), 1)
        at_x = row_of(position)
        at_y = position - PY * at_x
        level = 2 * vox + p + jnp.zeros((1, LANES), jnp.int32)
        norms = []
        for at, size in ((at_x, NX), (at_y, PY), (level, NZ)):
            norm = jnp.zeros((1, LANES), jnp.float32)
            for k in range(-RADIUS, RADIUS + 1):
                norm = norm + jnp.where((at + k >= 0) & (at + k < size), jnp.float32(WEIGHT[k]), 0.0)
            norms.append(norm)
        sums = total(p, EXTRA)
        sigma = jnp.sqrt(sums[1:2] / number / (norms[0] * norms[1] * norms[2]) + EPSILON)
        denominator = jnp.sqrt(number) * sigma
        observed = sums[0:1] / denominator
        best = jnp.full((GROUP, LANES), -1e30, jnp.float32)
        share = jnp.zeros((GROUP, LANES), jnp.float32)
        for g in range(CHUNKS):
            tflip = total(p, g) / denominator
            best = jnp.maximum(best, tflip)
            share = share + jax.nn.sigmoid(2.0 * (tflip - observed))
        gathered[p, piece, pl.ds(0, 1), :] = jnp.max(best, axis=0, keepdims=True)
        gathered[p, piece, pl.ds(1, 1), :] = jnp.sum(share, axis=0, keepdims=True) / NF

    for step in range(4):
        copies = []
        size = 1 << step
        for p in range(2):
            peer = [z_peer(1 - p), z_peer(p), y_peer(1 - p), y_peer(p)][step]
            place = gathered.at[p, pl.ds(owned[p] // size * size, size)]
            copies.append(pltpu.make_async_remote_copy(
                src_ref=place, dst_ref=place, send_sem=gather_send.at[step, p], recv_sem=gather_recv.at[step, p],
                device_id=peer, device_id_type=MESH,
            ))
        for copy in copies:
            copy.start()
        for copy in copies:
            copy.wait_recv()
        started.extend(copies)

    for i in range(PIECES):
        width = min(LANES, PLANE - LANES * i)
        for p in range(2):
            block_of = gathered[p, i]
            high_ref[pl.ds(p, 1), pl.ds(LANES * i, width)] = block_of[0:1, :width]
            exceed_ref[pl.ds(p, 1), pl.ds(LANES * i, width)] = block_of[1:2, :width]

    for copy in started + halo:
        copy.wait_send()


def per_device(contrasts, flips, mask):
    local, depth, cells = contrasts.shape
    f32 = jnp.float32
    vmem = pltpu.VMEM
    high, exceed = pl.pallas_call(
        kernel,
        out_shape=[jax.ShapeDtypeStruct((depth, cells), f32)] * 2,
        in_specs=[pl.BlockSpec(memory_space=pl.ANY), pl.BlockSpec(memory_space=vmem)],
        out_specs=[pl.BlockSpec(memory_space=vmem)] * 2,
        scratch_shapes=[
            vmem((local, 2, cells), jnp.bfloat16),
            vmem((2 * NF + 16, 2 * local), jnp.bfloat16),
            vmem((2, CHUNKS, PIECES, GROUP, LANES), f32),
            vmem((2, PIECES, 2, LANES), f32),
            *[vmem((2, CHUNKS, m, GROUP, LANES), f32) for m in (8, 4, 2, 1)],
            *[vmem((2, m, 2, LANES), f32) for m in (8, 4, 2, 1)],
            *[vmem((2, CHUNKS, m, GROUP, LANES), f32) for m in (4, 2, 1)],
            *[vmem((2, m, 2, LANES), f32) for m in (4, 2, 1)],
            vmem((2, WIDE + 2 * MARGIN), f32),
            vmem((2, WIDE + 2 * MARGIN), f32),
            vmem((2, WIDE), f32),
            vmem((2, WIDE), f32),
            vmem((2, WIDE), f32),
            vmem((2, PIECES, 2, LANES), f32),
            pltpu.SemaphoreType.DMA((8,)),
            pltpu.SemaphoreType.DMA((4, 2, CHUNKS + 1)),
            pltpu.SemaphoreType.DMA((4, 2, CHUNKS + 1)),
            pltpu.SemaphoreType.DMA((2,)),
            pltpu.SemaphoreType.DMA((2,)),
            pltpu.SemaphoreType.DMA((4, 2)),
            pltpu.SemaphoreType.DMA((4, 2)),
        ],
        compiler_params=pltpu.CompilerParams(
            collective_id=0, has_side_effects=True, vmem_limit_bytes=60 * 1024 * 1024
        ),
    )(contrasts, flips)
    inside = mask.astype(f32)
    return high * inside, exceed * inside


def solution(mesh):
    in_specs = (P("subj", "vox", None), P(None, "subj"), P("vox", None))
    out_specs = (P("vox", None), P("vox", None))
    return jax.shard_map(
        per_device, mesh=mesh, in_specs=in_specs, out_specs=out_specs, check_vma=False
    )
```

time: 460 us -> 90.9 us (0.20); the launches traced: 454 us -> 90.5 us
  waiting for transfers between devices: 402 us -> 0 us
  Pallas kernels: 0 us -> 88.2 us
  between operations: 14.2 us -> 0.65 us
  other arithmetic: 12.9 us -> 1.66 us
  local copies, waits for them, and re-layouts: 10.2 us -> 0.01 us
  matrix products: 8.38 us -> 0 us
  starting transfers between devices: 5.78 us -> 0 us
    psum x1 -> x0, waiting for transfers between devices: 401 us -> none  [per_device(): linear, second = lax.psum((linear, squared), 'subj')]
    pallas_call x0 -> x1, Pallas kernels: none -> 88.2 us  [per_device(): pl.pallas_call(kernel, out_shape=[jax.ShapeDtypeStruct((depth, cells), f3...]
    reshape x2 -> x0, local copies, waits for them, and re-layouts: 8.8 us -> none  [the longest x1 8.05 us: per_device(): values = contrasts.reshape(local_subjects, depth * plane_cells)]
    reduce_sum x2 -> x0, other arithmetic: 8.74 us -> none  [the longest x1 4.67 us: per_device(): squared = jnp.sum(jnp.square(values.astype(jnp.float32)), axis=0)]
    dot_general x4 -> x0, matrix products: 8.38 us -> none  [the longest x3 7.68 us: per_device(): jnp.dot(sign_rows, values, preferred_element_type=jnp.float32)]
    ppermute x2 -> x0, starting transfers between devices: 5.74 us -> none  [the longest x1 3.82 us: padded_2(): after = lax.ppermute(leading, axis, down)]
  transfers between devices with their start and end apart: 3 -> 0, of which waited for: 2 -> 0; matrix products, arithmetic and copies ran while one was open for 0% -> 0% of each run, Pallas kernels for 0% -> 0%
where the time goes in v1:
time: 90.9 us; the launch traced here: 90.5 us
  Pallas kernels  88.2 us (97%)
  other arithmetic  1.66 us (2%)
    pallas_call x1, Pallas kernels, per_device(): pl.pallas_call(kernel, out_shape=[jax.ShapeDtypeStruct((depth, cells), f3...  88.2 us

profile of v1, /device:TPU:6, one launch (start us, length us, event | category | flops | bytes accessed | tf_op | source)
XLA Modules:
  0.0 90.5 jit_solution(6951053240635979122)
XLA Ops:
  0.6 0.0 copy-start
  0.6 88.2 %shard_map.50 = (f32[2,9919]{1,0:T(2,128)}, f32[2,9919]{1,0:T(2,128)}) custom-call(bf16[112,2,9919]{2,1,0:T(2,128)(2,1)} %x_hbm.1, s32[48,112]{1,0:T(8,128)} %flips_ref.1), custom_call_target="tpu_custom_call" | custom-call | tf_op jit(solution)/shard_map/pallas_call | solution.py:346
  88.9 0.0 copy-done
  88.9 1.7 %convert_multiply_fusion = (f32[2,9919]{1,0:T(2,128)}, f32[2,9919]{1,0:T(2,128)}) fusion(f32[2,9919]{1,0:T(2,128)} %get-tuple-element.5, s32[2,9919]{1,0:T(2,128)S(1)} %copy-done, f32[2,9919]{1,0:T(2,128)} %get-tuple-element.4), kind=kLoop, calls=%fused_computation | loop fusion | flops 59514 | bytes 396760 | tf_op jit(solution)/shard_map/mul | solution.py:379
Async XLA Ops:
  0.6 88.2 %copy-start = (s32[2,9919]{1,0:T(2,128)S(1)}, s32[2,9919]{1,0:T(2,128)}, u32[]{:S(2)}) copy-start(s32[2,9919]{1,0:T(2,128)} %param.5) | copy-start | bytes 238060

commit v2 on v1

v2 whole, which is shorter than its diff:
```python
import functools
import math

import jax
import jax.numpy as jnp
from jax import lax
from jax.experimental import pallas as pl
from jax.experimental.pallas import tpu as pltpu
from jax.sharding import PartitionSpec as P

NX = 91
PY = 109
PLANE = NX * PY
NZ = 64
NF = 48
SUBJ = 1792
RADIUS = 2
EPSILON = 1e-06

TILE = 128
PIECES = 16
CHUNKS = 5
SPAN = TILE * PIECES
WIDE = SPAN * CHUNKS
LANES = TILE * CHUNKS
HALVES = 2
GROUP = NF // HALVES
ITEMS = CHUNKS * HALVES
EXTRA = ITEMS
BLOCK = 256
MARGIN = 256
SEG = 1280
ORDER = (0, 1, 2, 3, 4, 5, 6, EXTRA, 7, 8, 9)

WEIGHT = {k: math.exp(-0.5 * k * k) for k in range(-RADIUS, RADIUS + 1)}
MESH = pl.DeviceIdType.MESH


def row_of(position):
    return (position * 38480) >> 22


def first_bit(i):
    return ((i + 1) // 2) % 2


def second_bit(i):
    return i // 2


def partner(i, kind):
    odd = i % 2
    return (i + 1 - 2 * odd) if kind == 0 else (i + 3 + 2 * odd) % 4


def piece_of(p, y, z):
    bits = (first_bit, second_bit) if p == 0 else (second_bit, first_bit)
    return 8 * bits[0](y) + 4 * bits[1](y) + 2 * bits[0](z) + bits[1](z)


OWNER = [{piece_of(p, d // 4, d % 4): d for d in range(PIECES)} for p in range(2)]


def kernel(
    x_hbm, flips_ref, high_ref, exceed_ref,
    x, w, full, extra, r1, r2, r3, r4, e1, e2, e3, e4, s2, s3, s4, t2, t3, t4,
    square, swept, smooth, before, after, gathered,
    in_sem, send_sem, recv_sem, halo_send, halo_recv, gather_send, gather_recv,
):
    subj = lax.axis_index("subj")
    vox = lax.axis_index("vox")
    n_vox = lax.axis_size("vox")
    y, z = subj // 4, subj % 4
    up = (vox + 1) % n_vox
    down = (vox + n_vox - 1) % n_vox

    def y_peer(kind):
        return {"subj": partner(y, kind) * 4 + z}

    def z_peer(kind):
        return {"subj": y * 4 + partner(z, kind)}

    loads = []
    for c in range(CHUNKS):
        width = min(SPAN, PLANE - SPAN * c)
        view = (slice(None), slice(None), pl.ds(SPAN * c, width))
        load = pltpu.make_async_copy(x_hbm.at[view], x.at[view], in_sem.at[c])
        load.start()
        loads.append(load)

    barrier = pltpu.get_barrier_semaphore()
    for kind in range(2):
        pl.semaphore_signal(barrier, 1, device_id=y_peer(kind), device_id_type=MESH)
        pl.semaphore_signal(barrier, 1, device_id=z_peer(kind), device_id_type=MESH)
    for other in (up, down):
        pl.semaphore_signal(barrier, 1, device_id={"vox": other}, device_id_type=MESH)

    signs = flips_ref[...].astype(jnp.float32).astype(jnp.bfloat16)
    n_local = signs.shape[1]
    column = lax.broadcasted_iota(jnp.int32, (n_local, 2 * n_local), 1)
    subject = lax.broadcasted_iota(jnp.int32, (n_local, 2 * n_local), 0)
    for p in range(2):
        spread = (column == 2 * subject + p).astype(jnp.float32).astype(jnp.bfloat16)
        w[pl.ds(NF * p, NF), :] = jnp.dot(
            signs, spread, preferred_element_type=jnp.float32
        ).astype(jnp.bfloat16)
    lane = lax.broadcasted_iota(jnp.int32, (16, 2 * n_local), 1)
    line = lax.broadcasted_iota(jnp.int32, (16, 2 * n_local), 0)
    w[pl.ds(2 * NF, 16), :] = (lane % 2 == line).astype(jnp.float32).astype(jnp.bfloat16)

    def multiply(c):
        loads[c].wait()
        for start in range(SPAN * c, min(SPAN * (c + 1), PLANE), BLOCK):
            width = min(BLOCK, PLANE - start)
            values = x[:, :, pl.ds(start, width)].reshape(2 * n_local, width)
            sums = jnp.dot(w[...], values, preferred_element_type=jnp.float32)
            wide = values.astype(jnp.float32)
            squared = jnp.sum((wide * wide).reshape(n_local // 4, 8, width), axis=0)
            second = squared[0:2] + squared[2:4] + squared[4:6] + squared[6:8]
            square[:, pl.ds(MARGIN + start, width)] = second
            for low in range(0, width, TILE):
                size = min(TILE, width - low)
                piece = (start + low) // TILE - PIECES * c
                for p in range(2):
                    for h in range(HALVES):
                        row = NF * p + GROUP * h
                        full[p, c, h, piece, :, pl.ds(0, size)] = sums[row:row + GROUP, low:low + size]
                    row = 2 * NF + p
                    extra[p, piece, pl.ds(0, 1), pl.ds(TILE * c, size)] = sums[row:row + 1, low:low + size]

    keep = []
    for p in range(2):
        bits = (first_bit, second_bit) if p == 0 else (second_bit, first_bit)
        keep.append([bits[0](y), bits[1](y), bits[0](z), bits[1](z)])

    def views(p, item):
        if item == EXTRA:
            return [ref.at[p] for ref in (extra, e1, e2, e3, e4, t2, t3, t4)]
        at = (p, item // HALVES, item % HALVES)
        return [ref.at[at] for ref in (full, r1, r2, r3, r4, s2, s3, s4)]

    def send_of(step, p, item):
        held = views(p, item)
        source = [held[0].at[pl.ds(8 * (1 - keep[p][0]), 8)], held[5], held[6], held[7]][step]
        peer = [y_peer(p), y_peer(1 - p), z_peer(p), z_peer(1 - p)][step]
        return pltpu.make_async_remote_copy(
            src_ref=source, dst_ref=held[1 + step],
            send_sem=send_sem.at[step, p, item], recv_sem=recv_sem.at[step, p, item],
            device_id=peer, device_id_type=MESH,
        )

    started = {}

    def start(step, p, item):
        copy = send_of(step, p, item)
        copy.start()
        started[step, p, item] = copy

    def advance(step, item):
        for p in range(2):
            k1, k2, k3, k4 = keep[p]
            started[step, p, item].wait_recv()
            a, b1, b2, b3, _, o2, o3, o4 = views(p, item)
            if step == 0:
                for i in range(4):
                    at = 4 * (1 - k2) + i
                    o2[i] = a[8 * k1 + at] + b1[at]
            elif step == 1:
                for i in range(2):
                    at = 2 * (1 - k3) + i
                    o3[i] = a[8 * k1 + 4 * k2 + at] + b1[4 * k2 + at] + b2[at]
            else:
                at = 1 - k4
                o4[0] = a[8 * k1 + 4 * k2 + 2 * k3 + at] + b1[4 * k2 + 2 * k3 + at] + b2[2 * k3 + at] + b3[at]
            start(step + 1, p, item)

    def total(p, item):
        k1, k2, k3, k4 = keep[p]
        started[3, p, item].wait_recv()
        a, b1, b2, b3, b4 = views(p, item)[:5]
        return a[8 * k1 + 4 * k2 + 2 * k3 + k4] + b1[4 * k2 + 2 * k3 + k4] + b2[2 * k3 + k4] + b3[k4] + b4[0]

    def shifted(ref, base, offset):
        padded = ref[:, pl.ds(base, SEG + 2 * MARGIN)]
        return pltpu.roll(padded, (-offset) % (SEG + 2 * MARGIN), 1)[:, MARGIN:MARGIN + SEG]

    def in_plane():
        @pl.loop(0, WIDE // SEG)
        def _(i):
            base = pl.multiple_of(i * SEG, TILE)
            position = base + lax.broadcasted_iota(jnp.int32, (2, SEG), 1)
            at = position - PY * row_of(position)
            result = jnp.zeros((2, SEG), jnp.float32)
            for k in range(-RADIUS, RADIUS + 1):
                moved = shifted(square, base, k)
                inside = (at + k >= 0) & (at + k < PY)
                result = result + WEIGHT[k] * jnp.where(inside, moved, 0.0)
            swept[:, pl.ds(pl.multiple_of(base + MARGIN, TILE), SEG)] = result

        @pl.loop(0, WIDE // SEG)
        def _(i):
            base = pl.multiple_of(i * SEG, TILE)
            result = jnp.zeros((2, SEG), jnp.float32)
            for k in range(-RADIUS, RADIUS + 1):
                result = result + WEIGHT[k] * shifted(swept, base, k * PY)
            smooth[:, pl.ds(base, SEG)] = result

    halo = [
        pltpu.make_async_remote_copy(
            src_ref=smooth, dst_ref=target, send_sem=halo_send.at[i], recv_sem=halo_recv.at[i],
            device_id={"vox": other}, device_id_type=MESH,
        )
        for i, (target, other) in enumerate(((before, up), (after, down)))
    ]

    def depth():
        for copy in halo:
            copy.wait_recv()
        first = vox > 0
        last = vox < n_vox - 1
        for i in range(0, WIDE, SEG):
            place = pl.ds(i, SEG)
            lower = jnp.where(first, before[:, place], 0.0)
            upper = jnp.where(last, after[:, place], 0.0)
            own = smooth[:, place]
            rows = (
                WEIGHT[2] * lower[0:1] + WEIGHT[1] * lower[1:2] + own[0:1] + WEIGHT[1] * own[1:2] + WEIGHT[2] * upper[0:1],
                WEIGHT[2] * lower[1:2] + WEIGHT[1] * own[0:1] + own[1:2] + WEIGHT[1] * upper[0:1] + WEIGHT[2] * upper[1:2],
            )
            for low in range(0, SEG, TILE):
                tile = (i + low) // TILE
                for p in range(2):
                    extra[p, tile % PIECES, pl.ds(1, 1), pl.ds(TILE * (tile // PIECES), TILE)] = rows[p][:, low:low + TILE]

    multiply(0)
    pl.semaphore_wait(barrier, 6)
    for item in ORDER[:2]:
        for p in range(2):
            start(0, p, item)

    zeros = jnp.zeros((2, MARGIN), jnp.float32)
    square[:, pl.ds(0, MARGIN)] = zeros
    edge = PLANE // TILE * TILE
    square[:, pl.ds(MARGIN + edge, WIDE + MARGIN - edge)] = jnp.zeros((2, WIDE + MARGIN - edge), jnp.float32)
    swept[:, pl.ds(0, MARGIN)] = zeros
    swept[:, pl.ds(MARGIN + WIDE, MARGIN)] = zeros
    for p in range(2):
        for i in range(edge // TILE % PIECES, PIECES):
            for h in range(HALVES):
                full[p, CHUNKS - 1, h, i] = jnp.zeros((GROUP, TILE), jnp.float32)
            extra[p, i, pl.ds(0, 1), pl.ds(LANES - TILE, TILE)] = jnp.zeros((1, TILE), jnp.float32)
    multiply(1)

    n = len(ORDER)
    for t in range(n + 3):
        if t < n:
            advance(0, ORDER[t])
            if t + 2 < n:
                if ORDER[t + 2] == EXTRA:
                    depth()
                for p in range(2):
                    start(0, p, ORDER[t + 2])
        if 0 <= t - 1 < n:
            advance(1, ORDER[t - 1])
        if 0 <= t - 3 < n:
            advance(2, ORDER[t - 3])
        if t < 3:
            multiply(t + 2)
        elif t == 3:
            in_plane()
            for copy in halo:
                copy.start()

    number = jnp.float32(SUBJ)
    scales = []
    for p in range(2):
        k1, k2, k3, k4 = keep[p]
        piece = 8 * k1 + 4 * k2 + 2 * k3 + k4
        spot = lax.broadcasted_iota(jnp.int32, (1, LANES), 1)
        position = (PIECES * (spot >> 7) + piece) * TILE + (spot & 127)
        at_x = row_of(position)
        at_y = position - PY * at_x
        level = 2 * vox + p + jnp.zeros((1, LANES), jnp.int32)
        norms = []
        for at, size in ((at_x, NX), (at_y, PY), (level, NZ)):
            norm = jnp.zeros((1, LANES), jnp.float32)
            for k in range(-RADIUS, RADIUS + 1):
                norm = norm + jnp.where((at + k >= 0) & (at + k < size), jnp.float32(WEIGHT[k]), 0.0)
            norms.append(norm)
        sums = total(p, EXTRA)
        sigma = jnp.sqrt(sums[1:2] / number / (norms[0] * norms[1] * norms[2]) + EPSILON)
        denominator = jnp.sqrt(number) * sigma
        scales.append((denominator, sums[0:1] / denominator))

    def finish(c):
        place = slice(TILE * c, TILE * (c + 1))
        for p in range(2):
            denominator, observed = (scale[:, place] for scale in scales[p])
            best = jnp.full((GROUP, TILE), -1e30, jnp.float32)
            share = jnp.zeros((GROUP, TILE), jnp.float32)
            for h in range(HALVES):
                tflip = total(p, HALVES * c + h) / denominator
                best = jnp.maximum(best, tflip)
                share = share + jax.nn.sigmoid(2.0 * (tflip - observed))
            gathered[subj, c, pl.ds(2 * p, 1), :] = jnp.max(best, axis=0, keepdims=True)
            gathered[subj, c, pl.ds(2 * p + 1, 1), :] = jnp.sum(share, axis=0, keepdims=True) / NF

    returned = []

    def give(step, part):
        chunks = pl.ds(0, CHUNKS - 1) if part == 0 else pl.ds(CHUNKS - 1, 1)
        copies = []
        for d in range(1, 4):
            if step == 0:
                place = gathered.at[pl.ds(subj, 1), chunks]
                peer = {"subj": y * 4 + (z + d) % 4}
            else:
                place = gathered.at[pl.ds(4 * y, 4), chunks]
                peer = {"subj": (y + d) % 4 * 4 + z}
            copy = pltpu.make_async_remote_copy(
                src_ref=place, dst_ref=place,
                send_sem=gather_send.at[step, part, d - 1], recv_sem=gather_recv.at[step, part, d - 1],
                device_id=peer, device_id_type=MESH,
            )
            copy.start()
            copies.append(copy)
        returned.extend(copies)
        return copies

    def arrived(copies):
        for copy in copies:
            copy.wait_recv()

    def write(chunks):
        for c in chunks:
            for i in range(PIECES):
                begin = SPAN * c + TILE * i
                width = min(TILE, PLANE - begin)
                if width <= 0:
                    continue
                for p in range(2):
                    for kind, ref in enumerate((high_ref, exceed_ref)):
                        ref[pl.ds(p, 1), pl.ds(begin, width)] = gathered[OWNER[p][i], c, pl.ds(2 * p + kind, 1), pl.ds(0, width)]

    for c in range(CHUNKS - 1):
        finish(c)
    z_early = give(0, 0)
    finish(CHUNKS - 1)
    z_late = give(0, 1)
    arrived(z_early)
    y_early = give(1, 0)
    arrived(z_late)
    y_late = give(1, 1)
    arrived(y_early)
    write(range(CHUNKS - 1))
    arrived(y_late)
    write((CHUNKS - 1,))

    for copy in list(started.values()) + halo + returned:
        copy.wait_send()


def per_device(contrasts, flips, mask):
    local, depth, cells = contrasts.shape
    f32 = jnp.float32
    vmem = pltpu.VMEM
    high, exceed = pl.pallas_call(
        kernel,
        out_shape=[jax.ShapeDtypeStruct((depth, cells), f32)] * 2,
        in_specs=[pl.BlockSpec(memory_space=pl.ANY), pl.BlockSpec(memory_space=vmem)],
        out_specs=[pl.BlockSpec(memory_space=vmem)] * 2,
        scratch_shapes=[
            vmem((local, 2, cells), jnp.bfloat16),
            vmem((2 * NF + 16, 2 * local), jnp.bfloat16),
            vmem((2, CHUNKS, HALVES, PIECES, GROUP, TILE), f32),
            vmem((2, PIECES, 2, LANES), f32),
            *[vmem((2, CHUNKS, HALVES, m, GROUP, TILE), f32) for m in (8, 4, 2, 1)],
            *[vmem((2, m, 2, LANES), f32) for m in (8, 4, 2, 1)],
            *[vmem((2, CHUNKS, HALVES, m, GROUP, TILE), f32) for m in (4, 2, 1)],
            *[vmem((2, m, 2, LANES), f32) for m in (4, 2, 1)],
            vmem((2, WIDE + 2 * MARGIN), f32),
            vmem((2, WIDE + 2 * MARGIN), f32),
            vmem((2, WIDE), f32),
            vmem((2, WIDE), f32),
            vmem((2, WIDE), f32),
            vmem((PIECES, CHUNKS, 4, TILE), f32),
            pltpu.SemaphoreType.DMA((CHUNKS,)),
            pltpu.SemaphoreType.DMA((4, 2, ITEMS + 1)),
            pltpu.SemaphoreType.DMA((4, 2, ITEMS + 1)),
            pltpu.SemaphoreType.DMA((2,)),
            pltpu.SemaphoreType.DMA((2,)),
            pltpu.SemaphoreType.DMA((2, 2, 3)),
            pltpu.SemaphoreType.DMA((2, 2, 3)),
        ],
        compiler_params=pltpu.CompilerParams(
            collective_id=0, has_side_effects=True, vmem_limit_bytes=60 * 1024 * 1024
        ),
    )(contrasts, flips)
    inside = mask.astype(f32)
    return high * inside, exceed * inside


def solution(mesh):
    in_specs = (P("subj", "vox", None), P(None, "subj"), P("vox", None))
    out_specs = (P("vox", None), P("vox", None))
    return jax.shard_map(
        per_device, mesh=mesh, in_specs=in_specs, out_specs=out_specs, check_vma=False
    )
```

time: 90.9 us -> 81.3 us (0.89)
  the two profiles are of different devices: /device:TPU:6 before, /device:TPU:8 now
where the time goes in v2:
time: 81.3 us; the launch traced here: 81.1 us
  Pallas kernels  78.8 us (97%)
  other arithmetic  1.66 us (2%)
    pallas_call x1, Pallas kernels, per_device(): pl.pallas_call(kernel, out_shape=[jax.ShapeDtypeStruct((depth, cells), f3...  78.8 us
    mul x1, other arithmetic, per_device(): return (high * inside, exceed * inside)  1.66 us

profile of v2, /device:TPU:8, one launch (start us, length us, event | category | flops | bytes accessed | tf_op | source)
XLA Modules:
  0.0 81.1 jit_solution(6202474361364644342)
XLA Ops:
  0.6 0.0 copy-start
  0.6 78.8 %shard_map.50 = (f32[2,9919]{1,0:T(2,128)}, f32[2,9919]{1,0:T(2,128)}) custom-call(bf16[112,2,9919]{2,1,0:T(2,128)(2,1)} %x_hbm.1, s32[48,112]{1,0:T(8,128)} %flips_ref.1), custom_call_target="tpu_custom_call" | custom-call | tf_op jit(solution)/shard_map/pallas_call | solution.py:367
  79.4 0.0 copy-done
  79.4 1.7 %convert_multiply_fusion = (f32[2,9919]{1,0:T(2,128)}, f32[2,9919]{1,0:T(2,128)}) fusion(f32[2,9919]{1,0:T(2,128)} %get-tuple-element.5, s32[2,9919]{1,0:T(2,128)S(1)} %copy-done, f32[2,9919]{1,0:T(2,128)} %get-tuple-element.4), kind=kLoop, calls=%fused_computation | loop fusion | flops 59514 | bytes 396760 | tf_op jit(solution)/shard_map/mul | solution.py:400
Async XLA Ops:
  0.6 78.8 %copy-start = (s32[2,9919]{1,0:T(2,128)S(1)}, s32[2,9919]{1,0:T(2,128)}, u32[]{:S(2)}) copy-start(s32[2,9919]{1,0:T(2,128)} %param.5) | copy-start | bytes 238060

commit v3 on v2

--- a/solution.py
+++ b/solution.py
@@ -23,14 +23,19 @@
 SPAN = TILE * PIECES
 WIDE = SPAN * CHUNKS
 LANES = TILE * CHUNKS
-HALVES = 2
-GROUP = NF // HALVES
-ITEMS = CHUNKS * HALVES
+ROWS = ((24, 24), (24, 24), (24, 24), (24, 24), (24, 24))
+PARTS = [(c, sum(rows[:i]), rows[i]) for c, rows in enumerate(ROWS) for i in range(len(rows))]
+ITEMS = len(PARTS)
 EXTRA = ITEMS
 BLOCK = 256
 MARGIN = 256
 SEG = 1280
-ORDER = (0, 1, 2, 3, 4, 5, 6, EXTRA, 7, 8, 9)
+AHEAD = 2
+NEXT = 1
+WORK = 0
+LAG = 3
+ENTRY = 7
+ORDER = (*range(ENTRY), EXTRA, *range(ENTRY, ITEMS))
 
 WEIGHT = {k: math.exp(-0.5 * k * k) for k in range(-RADIUS, RADIUS + 1)}
 MESH = pl.DeviceIdType.MESH
@@ -66,6 +71,7 @@
     x, w, full, extra, r1, r2, r3, r4, e1, e2, e3, e4, s2, s3, s4, t2, t3, t4,
     square, swept, smooth, before, after, gathered,
     in_sem, send_sem, recv_sem, halo_send, halo_recv, gather_send, gather_recv,
+    flat_send, flat_recv,
 ):
     subj = lax.axis_index("subj")
     vox = lax.axis_index("vox")
@@ -122,9 +128,8 @@
                 size = min(TILE, width - low)
                 piece = (start + low) // TILE - PIECES * c
                 for p in range(2):
-                    for h in range(HALVES):
-                        row = NF * p + GROUP * h
-                        full[p, c, h, piece, :, pl.ds(0, size)] = sums[row:row + GROUP, low:low + size]
+                    row = NF * p
+                    full[p, c, piece, :, pl.ds(0, size)] = sums[row:row + NF, low:low + size]
                     row = 2 * NF + p
                     extra[p, piece, pl.ds(0, 1), pl.ds(TILE * c, size)] = sums[row:row + 1, low:low + size]
 
@@ -136,7 +141,8 @@
     def views(p, item):
         if item == EXTRA:
             return [ref.at[p] for ref in (extra, e1, e2, e3, e4, t2, t3, t4)]
-        at = (p, item // HALVES, item % HALVES)
+        c, row, rows = PARTS[item]
+        at = (p, c, slice(None), pl.ds(row, rows))
         return [ref.at[at] for ref in (full, r1, r2, r3, r4, s2, s3, s4)]
 
     def send_of(step, p, item):
@@ -234,7 +240,7 @@
 
     multiply(0)
     pl.semaphore_wait(barrier, 6)
-    for item in ORDER[:2]:
+    for item in ORDER[:AHEAD]:
         for p in range(2):
             start(0, p, item)
 
@@ -246,27 +252,26 @@
     swept[:, pl.ds(MARGIN + WIDE, MARGIN)] = zeros
     for p in range(2):
         for i in range(edge // TILE % PIECES, PIECES):
-            for h in range(HALVES):
-                full[p, CHUNKS - 1, h, i] = jnp.zeros((GROUP, TILE), jnp.float32)
+            full[p, CHUNKS - 1, i] = jnp.zeros((NF, TILE), jnp.float32)
             extra[p, i, pl.ds(0, 1), pl.ds(LANES - TILE, TILE)] = jnp.zeros((1, TILE), jnp.float32)
     multiply(1)
 
     n = len(ORDER)
-    for t in range(n + 3):
+    for t in range(n + LAG):
         if t < n:
             advance(0, ORDER[t])
-            if t + 2 < n:
-                if ORDER[t + 2] == EXTRA:
+            if t + AHEAD < n:
+                if ORDER[t + AHEAD] == EXTRA:
                     depth()
                 for p in range(2):
-                    start(0, p, ORDER[t + 2])
-        if 0 <= t - 1 < n:
-            advance(1, ORDER[t - 1])
-        if 0 <= t - 3 < n:
-            advance(2, ORDER[t - 3])
-        if t < 3:
-            multiply(t + 2)
-        elif t == 3:
+                    start(0, p, ORDER[t + AHEAD])
+        if 0 <= t - NEXT < n:
+            advance(1, ORDER[t - NEXT])
+        if 0 <= t - LAG < n:
+            advance(2, ORDER[t - LAG])
+        if WORK <= t < WORK + 3:
+            multiply(t - WORK + 2)
+        elif t == WORK + 3:
             in_plane()
             for copy in halo:
                 copy.start()
@@ -296,36 +301,35 @@
         place = slice(TILE * c, TILE * (c + 1))
         for p in range(2):
             denominator, observed = (scale[:, place] for scale in scales[p])
-            best = jnp.full((GROUP, TILE), -1e30, jnp.float32)
-            share = jnp.zeros((GROUP, TILE), jnp.float32)
-            for h in range(HALVES):
-                tflip = total(p, HALVES * c + h) / denominator
-                best = jnp.maximum(best, tflip)
-                share = share + jax.nn.sigmoid(2.0 * (tflip - observed))
+            best = jnp.full((8, TILE), -1e30, jnp.float32)
+            share = jnp.zeros((8, TILE), jnp.float32)
+            for item, part in enumerate(PARTS):
+                if part[0] == c:
+                    tflip = total(p, item) / denominator
+                    chance = jax.nn.sigmoid(2.0 * (tflip - observed))
+                    for low in range(0, part[2], 8):
+                        best = jnp.maximum(best, tflip[low:low + 8])
+                        share = share + chance[low:low + 8]
             gathered[subj, c, pl.ds(2 * p, 1), :] = jnp.max(best, axis=0, keepdims=True)
             gathered[subj, c, pl.ds(2 * p + 1, 1), :] = jnp.sum(share, axis=0, keepdims=True) / NF
 
     returned = []
 
-    def give(step, part):
-        chunks = pl.ds(0, CHUNKS - 1) if part == 0 else pl.ds(CHUNKS - 1, 1)
+    def give(place, peers, send, recv):
         copies = []
-        for d in range(1, 4):
-            if step == 0:
-                place = gathered.at[pl.ds(subj, 1), chunks]
-                peer = {"subj": y * 4 + (z + d) % 4}
-            else:
-                place = gathered.at[pl.ds(4 * y, 4), chunks]
-                peer = {"subj": (y + d) % 4 * 4 + z}
+        for d, peer in peers:
             copy = pltpu.make_async_remote_copy(
-                src_ref=place, dst_ref=place,
-                send_sem=gather_send.at[step, part, d - 1], recv_sem=gather_recv.at[step, part, d - 1],
-                device_id=peer, device_id_type=MESH,
+                src_ref=place, dst_ref=place, send_sem=send.at[d - 1], recv_sem=recv.at[d - 1],
+                device_id={"subj": peer}, device_id_type=MESH,
             )
             copy.start()
             copies.append(copy)
         returned.extend(copies)
         return copies
+
+    z_peers = [(d, y * 4 + (z + d) % 4) for d in (2, 1, 3)]
+    y_peers = [(d, (y + d) % 4 * 4 + z) for d in (2, 1, 3)]
+    early, late = pl.ds(0, CHUNKS - 1), pl.ds(CHUNKS - 1, 1)
 
     def arrived(copies):
         for copy in copies:
@@ -344,16 +348,17 @@
 
     for c in range(CHUNKS - 1):
         finish(c)
-    z_early = give(0, 0)
+    z_early = give(gathered.at[pl.ds(subj, 1), early], z_peers, gather_send.at[0], gather_recv.at[0])
     finish(CHUNKS - 1)
-    z_late = give(0, 1)
+    all_peers = [
+        (4 * e + d, (y + e) % 4 * 4 + (z + d) % 4) for d in (2, 1, 3, 0) for e in (2, 1, 3, 0) if d or e
+    ]
+    flat = give(gathered.at[pl.ds(subj, 1), late], all_peers, flat_send, flat_recv)
     arrived(z_early)
-    y_early = give(1, 0)
-    arrived(z_late)
-    y_late = give(1, 1)
+    y_early = give(gathered.at[pl.ds(4 * y, 4), early], y_peers, gather_send.at[1], gather_recv.at[1])
     arrived(y_early)
     write(range(CHUNKS - 1))
-    arrived(y_late)
+    arrived(flat)
     write((CHUNKS - 1,))
 
     for copy in list(started.values()) + halo + returned:
@@ -372,11 +377,11 @@
         scratch_shapes=[
             vmem((local, 2, cells), jnp.bfloat16),
             vmem((2 * NF + 16, 2 * local), jnp.bfloat16),
-            vmem((2, CHUNKS, HALVES, PIECES, GROUP, TILE), f32),
+            vmem((2, CHUNKS, PIECES, NF, TILE), f32),
             vmem((2, PIECES, 2, LANES), f32),
-            *[vmem((2, CHUNKS, HALVES, m, GROUP, TILE), f32) for m in (8, 4, 2, 1)],
+            *[vmem((2, CHUNKS, m, NF, TILE), f32) for m in (8, 4, 2, 1)],
             *[vmem((2, m, 2, LANES), f32) for m in (8, 4, 2, 1)],
-            *[vmem((2, CHUNKS, HALVES, m, GROUP, TILE), f32) for m in (4, 2, 1)],
+            *[vmem((2, CHUNKS, m, NF, TILE), f32) for m in (4, 2, 1)],
             *[vmem((2, m, 2, LANES), f32) for m in (4, 2, 1)],
             vmem((2, WIDE + 2 * MARGIN), f32),
             vmem((2, WIDE + 2 * MARGIN), f32),
@@ -389,8 +394,10 @@
             pltpu.SemaphoreType.DMA((4, 2, ITEMS + 1)),
             pltpu.SemaphoreType.DMA((2,)),
             pltpu.SemaphoreType.DMA((2,)),
-            pltpu.SemaphoreType.DMA((2, 2, 3)),
-            pltpu.SemaphoreType.DMA((2, 2, 3)),
+            pltpu.SemaphoreType.DMA((2, 3)),
+            pltpu.SemaphoreType.DMA((2, 3)),
+            pltpu.SemaphoreType.DMA((PIECES - 1,)),
+            pltpu.SemaphoreType.DMA((PIECES - 1,)),
         ],
         compiler_params=pltpu.CompilerParams(
             collective_id=0, has_side_effects=True, vmem_limit_bytes=60 * 1024 * 1024

time: 81.3 us -> 79.1 us (0.973)
  the two profiles are of different devices: /device:TPU:8 before, /device:TPU:6 now
where the time goes in v3:
time: 79.1 us; the launch traced here: 78.5 us
  Pallas kernels  76.1 us (96%)
  other arithmetic  1.66 us (2%)
    pallas_call x1, Pallas kernels, per_device(): pl.pallas_call(kernel, out_shape=[jax.ShapeDtypeStruct((depth, cells), f3...  76.1 us
    mul x1, other arithmetic, per_device(): return (high * inside, exceed * inside)  1.66 us

profile of v3, /device:TPU:6, one launch (start us, length us, event | category | flops | bytes accessed | tf_op | source)
XLA Modules:
  0.0 78.5 jit_solution(7337984209442620973)
XLA Ops:
  0.6 0.0 copy-start
  0.6 76.1 %shard_map.50 = (f32[2,9919]{1,0:T(2,128)}, f32[2,9919]{1,0:T(2,128)}) custom-call(bf16[112,2,9919]{2,1,0:T(2,128)(2,1)} %x_hbm.1, s32[48,112]{1,0:T(8,128)} %flips_ref.1), custom_call_target="tpu_custom_call" | custom-call | tf_op jit(solution)/shard_map/pallas_call | solution.py:372
  76.8 0.0 copy-done
  76.8 1.7 %convert_multiply_fusion = (f32[2,9919]{1,0:T(2,128)}, f32[2,9919]{1,0:T(2,128)}) fusion(f32[2,9919]{1,0:T(2,128)} %get-tuple-element.5, s32[2,9919]{1,0:T(2,128)S(1)} %copy-done, f32[2,9919]{1,0:T(2,128)} %get-tuple-element.4), kind=kLoop, calls=%fused_computation | loop fusion | flops 59514 | bytes 396760 | tf_op jit(solution)/shard_map/mul | solution.py:407
Async XLA Ops:
  0.6 76.2 %copy-start = (s32[2,9919]{1,0:T(2,128)S(1)}, s32[2,9919]{1,0:T(2,128)}, u32[]{:S(2)}) copy-start(s32[2,9919]{1,0:T(2,128)} %param.5) | copy-start | bytes 238060

commit v4 on v3

--- a/solution.py
+++ b/solution.py
@@ -32,9 +32,9 @@
 SEG = 1280
 AHEAD = 2
 NEXT = 1
-WORK = 0
+READY = 2
 LAG = 3
-ENTRY = 7
+ENTRY = 5
 ORDER = (*range(ENTRY), EXTRA, *range(ENTRY, ITEMS))
 
 WEIGHT = {k: math.exp(-0.5 * k * k) for k in range(-RADIUS, RADIUS + 1)}
@@ -238,7 +238,8 @@
                 for p in range(2):
                     extra[p, tile % PIECES, pl.ds(1, 1), pl.ds(TILE * (tile // PIECES), TILE)] = rows[p][:, low:low + TILE]
 
-    multiply(0)
+    for c in range(READY):
+        multiply(c)
     pl.semaphore_wait(barrier, 6)
     for item in ORDER[:AHEAD]:
         for p in range(2):
@@ -254,7 +255,11 @@
         for i in range(edge // TILE % PIECES, PIECES):
             full[p, CHUNKS - 1, i] = jnp.zeros((NF, TILE), jnp.float32)
             extra[p, i, pl.ds(0, 1), pl.ds(LANES - TILE, TILE)] = jnp.zeros((1, TILE), jnp.float32)
-    multiply(1)
+    for c in range(READY, CHUNKS):
+        multiply(c)
+    in_plane()
+    for copy in halo:
+        copy.start()
 
     n = len(ORDER)
     for t in range(n + LAG):
@@ -269,12 +274,6 @@
             advance(1, ORDER[t - NEXT])
         if 0 <= t - LAG < n:
             advance(2, ORDER[t - LAG])
-        if WORK <= t < WORK + 3:
-            multiply(t - WORK + 2)
-        elif t == WORK + 3:
-            in_plane()
-            for copy in halo:
-                copy.start()
 
     number = jnp.float32(SUBJ)
     scales = []

time: 79.1 us -> 78.4 us (level)
  no operation moved by 1% of the time
where the time goes in v4:
time: 78.4 us; the launch traced here: 78.2 us
  Pallas kernels  75.9 us (97%)
  other arithmetic  1.66 us (2%)
    pallas_call x1, Pallas kernels, per_device(): pl.pallas_call(kernel, out_shape=[jax.ShapeDtypeStruct((depth, cells), f3...  75.9 us
    mul x1, other arithmetic, per_device(): return (high * inside, exceed * inside)  1.66 us

profile of v4, /device:TPU:6, one launch (start us, length us, event | category | flops | bytes accessed | tf_op | source)
XLA Modules:
  0.0 78.2 jit_solution(5354711256335845310)
XLA Ops:
  0.6 0.0 copy-start
  0.6 75.9 %shard_map.50 = (f32[2,9919]{1,0:T(2,128)}, f32[2,9919]{1,0:T(2,128)}) custom-call(bf16[112,2,9919]{2,1,0:T(2,128)(2,1)} %x_hbm.1, s32[48,112]{1,0:T(8,128)} %flips_ref.1), custom_call_target="tpu_custom_call" | custom-call | tf_op jit(solution)/shard_map/pallas_call | solution.py:371
  76.5 0.0 copy-done
  76.5 1.7 %convert_multiply_fusion = (f32[2,9919]{1,0:T(2,128)}, f32[2,9919]{1,0:T(2,128)}) fusion(f32[2,9919]{1,0:T(2,128)} %get-tuple-element.5, s32[2,9919]{1,0:T(2,128)S(1)} %copy-done, f32[2,9919]{1,0:T(2,128)} %get-tuple-element.4), kind=kLoop, calls=%fused_computation | loop fusion | flops 59514 | bytes 396760 | tf_op jit(solution)/shard_map/mul | solution.py:406
Async XLA Ops:
  0.6 75.9 %copy-start = (s32[2,9919]{1,0:T(2,128)S(1)}, s32[2,9919]{1,0:T(2,128)}, u32[]{:S(2)}) copy-start(s32[2,9919]{1,0:T(2,128)} %param.5) | copy-start | bytes 238060
